TPU v7x, 256 devices: a whole 4x4x8 slice. The times are simulated.
256 devices in a mesh: dp: 4 (over x), context: 16 (over y_lo, z), tensor: 4 (over y_hi, core).
Axes of the slice: x: 4, y: 4 (y_hi: 2, y_lo: 2; y = y_hi * 2 + y_lo), z: 8, core: 2. Of those that a mesh axis runs over, the one named last changes fastest.
Arguments:
- grad_out: bfloat16 [32768, 8192], P(('dp', 'context', 'tensor')), may hold values from -24 to 24
- queries: bfloat16 [32768, 1024], P(('dp', 'context'), 'tensor'), may hold values from -6 to 6
- attended: bfloat16 [32768, 1024], P(('dp', 'context'), 'tensor'), may hold values from -6 to 6
- keys: bfloat16 [32768, 128], P(('dp', 'context')), may hold values from -6 to 6
- values: bfloat16 [32768, 128], P(('dp', 'context')), may hold values from -6 to 6
- log_sums: float32 [8, 32768], P('tensor', ('dp', 'context')), may hold values from 1 to 3
- segment_ids: int32 [4, 8192], P('dp'), may hold values from 0 to 7, as said below
- w_out: bfloat16 [8192, 1024], P(('dp', 'context'), 'tensor'), may hold values from -0.0625 to 0.0625
- w_query: bfloat16 [1024, 8192], P('tensor', ('dp', 'context')), may hold values from -0.1875 to 0.1875
- w_key: bfloat16 [128, 8192], replicated, may hold values from -0.5 to 0.5
- w_value: bfloat16 [128, 8192], replicated, may hold values from -0.5 to 0.5
Outputs:
- grad_input: bfloat16 [32768, 8192], P(('dp', 'context', 'tensor'))
- out_proj_grad: float32 [8192, 1024], P(('dp', 'context'), 'tensor')
Inputs may be any that keep to these rules, and one draw needn't show every extreme that they name: `segment_ids`: along the positions of a sequence the document number never falls; every sequence holds exactly 8 documents, numbered from 0.
All inputs are finite; a program needn't handle non-finite values.
Results may differ from a plain program's by a relative error of at most 0.02.
Values may be sent and summed in bfloat16 or wider, within the bound.
A program may use at most 128 MiB of HBM per device.

v0:
```python
import math

import jax
import jax.numpy as jnp
from jax import lax
from jax.sharding import PartitionSpec as P


def extended_2(x, sides, width):
    for axis, dim in sides:
        peers, length = (lax.axis_size(axis), x.shape[dim])
        up = [(i, (i + 1) % peers) for i in range(peers - 1)]
        down = [(j, i) for i, j in up]
        last = lax.slice_in_dim(x, length - width, length, axis=dim)
        initial = lax.slice_in_dim(x, 0, width, axis=dim)
        before = lax.ppermute(last, axis, up)
        after = lax.ppermute(initial, axis, down)
        x = jnp.concatenate([before, x, after], axis=dim)
    return x


def on_device(
    grad_out, queries, attended, keys, values, log_sums, segment_ids, w_out, w_query, w_key, w_value
):
    token_grads = lax.all_gather(grad_out, "tensor", axis=0, tiled=True)
    out_full, query_full = (
        lax.all_gather(w_out, ("dp", "context"), axis=0, tiled=True),
        lax.all_gather(w_query, ("dp", "context"), axis=1, tiled=True),
    )
    attn_grads = jnp.dot(token_grads, out_full, preferred_element_type=jnp.float32).astype(
        jnp.bfloat16
    )
    out_proj_grad = lax.psum_scatter(
        lax.dot_general(
            token_grads, attended, (((0,), (0,)), ((), ())), preferred_element_type=jnp.float32
        ),
        ("dp", "context"),
        scatter_dimension=0,
        tiled=True,
    )
    span_len = queries.shape[0] // 2
    head_dim = keys.shape[1]
    heads_here = queries.shape[1] // head_dim
    inv_root = 1.0 / math.sqrt(head_dim)
    cycle_size = lax.axis_size("context")
    cycle_pos = lax.axis_index("context")
    high_span = 2 * cycle_size - 1 - cycle_pos
    last_rank = cycle_pos == cycle_size - 1
    kv_pair = jnp.concatenate([keys, values], axis=1)
    flipped = jnp.concatenate([kv_pair[span_len:], kv_pair[:span_len]], axis=0)
    extended = extended_2(flipped, (("context", 0),), span_len)
    left_low = extended[:span_len]
    right_high = extended[3 * span_len :]
    own_low = kv_pair[:span_len]
    own_high = kv_pair[span_len:]
    prev_high = jnp.where(last_rank, own_low, right_high)
    block_kv = jnp.stack(
        [
            jnp.concatenate([left_low, own_low], axis=0),
            jnp.concatenate([prev_high, own_high], axis=0),
        ]
    )
    key_blk = block_kv[:, :, :head_dim]
    value_blk = block_kv[:, :, head_dim:]
    offsets = jnp.arange(span_len, dtype=jnp.int32)
    query_spans = jnp.stack([cycle_pos, high_span])
    query_pos = query_spans[:, None] * span_len + offsets[None, :]
    key_pos = jnp.concatenate([query_pos - span_len, query_pos], axis=1)
    seg_row = segment_ids[0]

    def seg_slice(span_idx):
        return lax.dynamic_slice_in_dim(seg_row, jnp.maximum(span_idx, 0) * span_len, span_len)

    seg_query = jnp.stack([seg_slice(cycle_pos), seg_slice(high_span)])
    seg_key = jnp.stack(
        [
            jnp.concatenate([seg_slice(cycle_pos - 1), seg_query[0]]),
            jnp.concatenate([seg_slice(high_span - 1), seg_query[1]]),
        ]
    )
    allowed = (
        (key_pos[:, None, :] <= query_pos[:, :, None])
        & (key_pos[:, None, :] >= 0)
        & (seg_key[:, None, :] == seg_query[:, :, None])
    )
    query_blk = queries.reshape(2, span_len, heads_here, head_dim)
    dout_blk = attn_grads.reshape(2, span_len, heads_here, head_dim)
    log_rows = log_sums.reshape(heads_here, 2, span_len).transpose(1, 0, 2)
    row_delta = (
        (attn_grads.astype(jnp.float32) * attended.astype(jnp.float32))
        .reshape(2, span_len, heads_here, head_dim)
        .sum(axis=3)
    )
    row_delta = row_delta.transpose(0, 2, 1)
    scores = (
        jnp.einsum("bqhe,bke->bhqk", query_blk, key_blk, preferred_element_type=jnp.float32)
        * inv_root
    )
    prob_full = jnp.where(allowed[:, None], jnp.exp(scores - log_rows[..., None]), 0.0)
    prob_low = prob_full.astype(jnp.bfloat16)
    dprobs = jnp.einsum("bqhe,bke->bhqk", dout_blk, value_blk, preferred_element_type=jnp.float32)
    dscores = (prob_full * (dprobs - row_delta[..., None])).astype(jnp.bfloat16)
    dquery = (
        jnp.einsum("bhqk,bke->bqhe", dscores, key_blk, preferred_element_type=jnp.float32)
        * inv_root
    ).astype(jnp.bfloat16)
    key_grads = (
        jnp.einsum("bhqk,bqhe->bke", dscores, query_blk, preferred_element_type=jnp.float32)
        * inv_root
    )
    value_grads = jnp.einsum(
        "bhqk,bqhe->bke", prob_low, dout_blk, preferred_element_type=jnp.float32
    )
    kv_block_grads = jnp.concatenate([key_grads, value_grads], axis=2)
    to_left = kv_block_grads[0, :span_len]
    to_right = jnp.where(last_rank, 0.0, kv_block_grads[1, :span_len])
    own_low_grads = kv_block_grads[0, span_len:] + jnp.where(
        last_rank, kv_block_grads[1, :span_len], 0.0
    )
    returned = extended_2(
        jnp.concatenate([to_left, to_right], axis=0).astype(jnp.bfloat16),
        (("context", 0),),
        span_len,
    ).astype(jnp.float32)
    low_summed = own_low_grads + returned[3 * span_len :]
    high_summed = kv_block_grads[1, span_len:] + returned[:span_len]
    kv_grads = jnp.concatenate([low_summed, high_summed], axis=0).astype(jnp.bfloat16)
    query_grads = dquery.reshape(2 * span_len, heads_here * head_dim)
    summed = jnp.dot(query_grads, query_full, preferred_element_type=jnp.float32)
    summed = summed + jnp.dot(kv_grads[:, :head_dim], w_key, preferred_element_type=jnp.float32)
    summed = summed + jnp.dot(kv_grads[:, head_dim:], w_value, preferred_element_type=jnp.float32)
    grad_input = lax.psum_scatter(
        summed.astype(jnp.bfloat16), "tensor", scatter_dimension=0, tiled=True
    )
    return (grad_input, out_proj_grad)


def solution(mesh):
    placed = (
        P(("dp", "context", "tensor"), None),
        P(("dp", "context"), "tensor"),
        P(("dp", "context"), "tensor"),
        P(("dp", "context"), None),
        P(("dp", "context"), None),
        P("tensor", ("dp", "context")),
        P("dp", None),
        P(("dp", "context"), "tensor"),
        P("tensor", ("dp", "context")),
        P(),
        P(),
    )
    return jax.shard_map(
        on_device,
        mesh=mesh,
        in_specs=placed,
        out_specs=(P(("dp", "context", "tensor"), None), P(("dp", "context"), "tensor")),
        check_vma=False,
    )
```

profile of v0, /device:TPU:8, one launch (start us, length us, event | category | flops | bytes accessed | tf_op | source)
XLA Modules:
  0.0 1044.4 jit_solution(14858236684178391399)
XLA Ops:
  9.4 67.3 %all-gather.4.cloned.1.call-done = bf16[512,8192]{1,0:T(8,128)(2,1)} async-done(((bf16[128,8192]{1,0:T(8,128)(2,1)}), bf16[512,8192]{1,0:T(8,128)(2,1)}) %all-gather.4.cloned.1.call-update) | async-done | bytes 8388624 | tf_op jit(solution)/shard_map/all_gather | solution.py:25
  76.7 9.0 fusion.40
  86.8 6.1 collective-permute-start.1
  93.8 2.9 collective-permute-done.1
  96.8 1.9 collective-permute-start
  98.7 1.2 compare_and_fusion
  100.2 6.5 collective-permute-done
  106.7 2.9 fusion.3
  109.6 261.7 %all-gather.6.cloned.1.call-done = bf16[8192,256]{1,0:T(8,128)(2,1)} async-done(((bf16[128,256]{1,0:T(8,128)(2,1)}), bf16[8192,256]{1,0:T(8,128)(2,1)}) %all-gather.6.cloned.1.call-update) | async-done | bytes 4194320 | tf_op jit(solution)/shard_map/all_gather | solution.py:27
  371.3 7.9 convert_multiply_fusion
  379.2 1.3 reshape.107
  382.4 2.2 convolution_bitcast_fusion
  385.1 1.4 fusion.4
  387.2 1.9 collective-permute-start.2
  389.1 6.2 collective-permute-start.3
  395.4 2.0 fusion.6
  397.3 1.1 copy.38
  398.4 1.1 fusion.16
  399.5 8.1 fusion.30
  407.6 8.1 fusion.28
  415.7 209.5 %all-gather.8.cloned.1.call-done = bf16[256,8192]{1,0:T(8,128)(2,1)} async-done(((bf16[256,128]{1,0:T(8,128)(2,1)}), bf16[256,8192]{1,0:T(8,128)(2,1)}) %all-gather.8.cloned.1.call-update) | async-done | bytes 4194320 | tf_op jit(solution)/shard_map/all_gather | solution.py:28
  625.3 16.6 %add_convert_fusion = bf16[512,8192]{1,0:T(8,128)(2,1)} fusion(f32[512,8192]{1,0:T(8,128)} %fusion.30, f32[512,8192]{1,0:T(8,128)} %fusion.28, bf16[256,8192]{1,0:T(8,128)(2,1)} %all-gather.8.cloned.1.call-done, bf16[64,8,2,128]{3,2,1,0:T(2,128)(2,1)S(1)} %bitcast.86), kind=kOutput, calls=%fused_computation | convolution fusion | flops 2160066560 | bytes 46399488 | tf_op jit(solution)/shard_map/dot_general | solution.py:129
  641.9 300.7 %reduce-scatter.5.cloned.1.call-done = f32[128,256]{1,0:T(8,128)} async-done(((f32[8192,256]{1,0:T(8,128)}), f32[128,256]{1,0:T(8,128)}) %reduce-scatter.5.cloned.1.call-update) | async-done | bytes 131088 | tf_op jit(solution)/shard_map/reduce_scatter | solution.py:33
  942.5 95.3 %reduce-scatter.3.cloned.1.call-done = bf16[128,8192]{1,0:T(8,128)(2,1)} async-done(((bf16[512,8192]{1,0:T(8,128)(2,1)}), bf16[128,8192]{1,0:T(8,128)(2,1)}) %reduce-scatter.3.cloned.1.call-update) | async-done | bytes 2097168 | tf_op jit(solution)/shard_map/reduce_scatter | solution.py:132
  (54 shorter events, 7.4 us)
Async XLA Ops:
  7.2 392.4 %copy-start = (bf16[128,8192]{1,0:T(8,128)(2,1)S(1)}, bf16[128,8192]{1,0:T(8,128)(2,1)}, u32[]{:S(2)}) copy-start(bf16[128,8192]{1,0:T(8,128)(2,1)} %param.21) | copy-start | bytes 6291460
  7.2 69.6 %all-gather.4.cloned.1.call-start = ((), (), s32[]{:S(2)}) async-start(), calls=%async_computation.2 | async-start | bytes 10485760 | tf_op jit(solution)/shard_map/all_gather | solution.py:25
  7.9 363.4 %all-gather.6.cloned.1.call-start = ((), (), s32[]{:S(2)}) async-start(), calls=%async_computation.3 | async-start | bytes 4259840 | tf_op jit(solution)/shard_map/all_gather | solution.py:27
  8.7 616.6 %all-gather.8.cloned.1.call-start = ((), (), s32[]{:S(2)}) async-start(), calls=%async_computation.4 | async-start | bytes 4259840 | tf_op jit(solution)/shard_map/all_gather | solution.py:28
  9.4 933.1 %reduce-scatter.5.cloned.1.call-start = ((), (), s32[]{:S(2)}) async-start(), calls=%async_computation.6 | async-start | bytes 8519680 | tf_op jit(solution)/shard_map/reduce_scatter | solution.py:33
  85.8 0.9 copy-start.7
  85.8 1.0 copy-start.8
  85.8 14.2 %copy-start.6 = (bf16[512,256]{1,0:T(8,128)(2,1)S(1)}, bf16[512,256]{1,0:T(8,128)(2,1)}, u32[]{:S(2)}) copy-start(bf16[512,256]{1,0:T(8,128)(2,1)} %param.12) | copy-start | bytes 786436
  85.8 20.9 %copy-start.9 = (f32[2,512]{1,0:T(2,128)S(1)}, f32[2,512]{1,0:T(2,128)}, u32[]{:S(2)}) copy-start(f32[2,512]{1,0:T(2,128)} %param.16) | copy-start | bytes 12292
  85.8 952.1 %reduce-scatter.3.cloned.1.call-start = ((), (), s32[]{:S(2)}) async-start(), calls=%async_computation.5 | async-start | bytes 10485760 | tf_op jit(solution)/shard_map/reduce_scatter | solution.py:132
  86.8 10.0 collective-permute-start.1
  96.8 9.9 collective-permute-start
  100.2 279.0 %copy-start.5 = (bf16[2,256,2,128]{1,3,2,0:T(8,128)(2,1)}, bf16[2,256,2,128]{1,3,2,0:T(8,128)(2,1)S(1)}, u32[]{:S(2)}) copy-start(bf16[2,256,2,128]{1,3,2,0:T(8,128)(2,1)S(1)} %copy.40) | copy-start | bytes 786436
  106.7 278.0 %copy-start.3 = (bf16[1,512,256]{2,1,0:T(8,128)(2,1)}, bf16[1,512,256]{2,1,0:T(8,128)(2,1)S(1)}, u32[]{:S(2)}) copy-start(bf16[1,512,256]{2,1,0:T(8,128)(2,1)S(1)} %maximum_bitcast_fusion) | copy-start | bytes 786436
  382.4 2.2 copy-start.2
  387.2 11.2 %collective-permute-start.2 = (bf16[256,256]{0,1:T(8,128)(2,1)S(1)}, bf16[256,256]{0,1:T(8,128)(2,1)}, u32[]{:S(2)}, u32[]{:S(2)}) collective-permute-start(bf16[256,256]{0,1:T(8,128)(2,1)S(1)} %get-tuple-element.4), channel_id=1, source_target_pairs={{0,4},{4,8},{8,12},{12,16},{16,20},{20,24},{24,28},{28,32},{32,36}... | collective-permute-start | bytes 393224 | tf_op jit(solution)/shard_map/ppermute | solution.py:16
  389.1 9.3 collective-permute-start.3
  399.5 8.1 copy-start.4
  641.8 396.0 %copy-start.1 = (bf16[128,8192]{1,0:T(8,128)(2,1)S(1)}, bf16[128,8192]{1,0:T(8,128)(2,1)}, u32[]{:S(2)}) copy-start(bf16[128,8192]{1,0:T(8,128)(2,1)} %param.21) | copy-start | bytes 6291460
Sparse Core Ops, SparseCore 0:
  9.8 66.8 all-gather.3
  78.5 292.7 all-gather.5
  373.0 252.1 all-gather.7
  628.2 314.2 reduce-scatter.4
  945.8 92.0 reduce-scatter.2
where the time goes:
time: 1050 us; the launch traced here: 1040 us
  waiting for transfers between devices  946 us (90%)
  matrix products  58.6 us (6%)
  starting transfers between devices  16.3 us (2%)
  between operations  14 us (1%)
    reduce_scatter x1, waiting for transfers between devices, on_device(): lax.psum_scatter(lax.dot_general(token_grads, attended, (((0,), (0,)), ((...  301 us
    all_gather x1, waiting for transfers between devices, on_device(): lax.all_gather(w_out, ('dp', 'context'), axis=0, tiled=True)  262 us
    all_gather x1, waiting for transfers between devices, on_device(): lax.all_gather(w_query, ('dp', 'context'), axis=1, tiled=True)  210 us
    reduce_scatter x1, waiting for transfers between devices, on_device(): lax.psum_scatter(summed.astype(jnp.bfloat16), 'tensor', scatter_dimension...  95.3 us
    all_gather x1, waiting for transfers between devices, on_device(): token_grads = lax.all_gather(grad_out, 'tensor', axis=0, tiled=True)  67.3 us
  transfers between devices with their start and end apart: 9, of which 7 were waited for; matrix products, arithmetic and copies ran while one was open for 6% of the time, Pallas kernels for 0%

commit v1 on v0

v1 whole, which is shorter than its diff:
```python
import functools
import math

import jax
import jax.numpy as jnp
from jax import lax
from jax.experimental import pallas as pl
from jax.experimental.pallas import tpu as pltpu
from jax.sharding import PartitionSpec as P

MESH = pl.DeviceIdType.MESH
BF = jnp.bfloat16
F32 = jnp.float32
NX, NY, NZ = 4, 4, 8
SPAN = 256
HD = 128
N_REMOTE = 200
N_LOCAL = 8


def wrap(i, n):
    return lax.rem(i + n, n)


class Links:
    def __init__(self, send, recv):
        self.send, self.recv, self.started = send, recv, []

    def copy(self, src, dst, dev):
        n = len(self.started)
        c = pltpu.make_async_remote_copy(
            src_ref=src,
            dst_ref=dst,
            send_sem=self.send.at[n],
            recv_sem=self.recv.at[n],
            device_id=dev,
            device_id_type=MESH,
        )
        c.start()
        self.started.append(c)
        return c


def ring_gather(links, n, i, slab, half, up, down, arrived=None):
    k = n // 2
    cp = links.copy(slab(i), slab(i), up)
    cm = links.copy(slab(i), slab(i), down)
    if arrived is not None:
        arrived(slab(i))
    yield
    for s in range(1, k):
        before, after = wrap(i - s, n), wrap(i + s, n)
        cp.wait_recv()
        got = slab(before)
        piece = got if s < k - 1 else got.at[0:half]
        cp = links.copy(piece, piece, up)
        if arrived is not None:
            arrived(got)
        cm.wait_recv()
        got = slab(after)
        piece = got if s < k - 1 else got.at[half : 2 * half]
        cm = links.copy(piece, piece, down)
        if arrived is not None:
            arrived(got)
        yield
    cp.wait_recv()
    cm.wait_recv()
    if arrived is not None:
        arrived(slab(wrap(i + k, n)))


def ring_reduce(links, n, i, slab, buf, half, up, down):
    k = n // 2
    far = wrap(i + k, n)
    cp = links.copy(slab(far).at[0:half], buf.at[0, 0, 0:half], up)
    cm = links.copy(slab(far).at[half : 2 * half], buf.at[1, 0, half : 2 * half], down)
    yield

    def add(dst, part):
        dst[...] = (dst[...].astype(F32) + part[...].astype(F32)).astype(BF)

    for step in range(1, k):
        s = k - step
        dst = slab(wrap(i + s, n))
        cp.wait_recv()
        if step == 1:
            add(dst.at[0:half], buf.at[0, 0, 0:half])
        else:
            add(dst, buf.at[0, step - 1])
        cp = links.copy(dst, buf.at[0, step], up)
        dst = slab(wrap(i - s, n))
        cm.wait_recv()
        if step == 1:
            add(dst.at[half : 2 * half], buf.at[1, 0, half : 2 * half])
        else:
            add(dst, buf.at[1, step - 1])
        cm = links.copy(dst, buf.at[1, step], down)
        yield
    cp.wait_recv()
    cm.wait_recv()
    dst = slab(i)
    dst[...] = (
        dst[...].astype(F32) + buf[0, k - 1].astype(F32) + buf[1, k - 1].astype(F32)
    ).astype(BF)


def contract(a, b, da, db):
    return lax.dot_general(a, b, (((da,), (db,)), ((), ())), preferred_element_type=F32)


def kernel(
    grad_out, queries, attended, keys, values, log_sums, seg, w_out, w_query, w_key, w_value,
    gin, dwo,
    tg, fwd, wv, qv, kvw, pb, raz, rax, ray, rbx, rbz, rby,
    halo, ag, att_t, acc, qkv, kvg, kvback, kvland, ab, send, recv, loc,
):
    x = lax.axis_index("dp")
    r = lax.axis_index("context")
    t = lax.axis_index("tensor")
    yl, z = lax.div(r, NZ), lax.rem(r, NZ)
    yh, core = lax.div(t, 2), lax.rem(t, 2)
    y = 2 * yh + yl
    other = 1 - core
    partner = 2 * (1 - yh) + core

    def dev(x, y, z, core):
        return {
            "dp": x,
            "context": lax.rem(y, 2) * NZ + z,
            "tensor": lax.div(y, 2) * 2 + core,
        }

    xp, xm = dev(wrap(x + 1, NX), y, z, core), dev(wrap(x - 1, NX), y, z, core)
    yp, ym = dev(x, wrap(y + 1, NY), z, core), dev(x, wrap(y - 1, NY), z, core)
    zp, zm = dev(x, y, wrap(z + 1, NZ), core), dev(x, y, wrap(z - 1, NZ), core)
    pair = dev(x, 2 * yh + 1 - yl, z, core)
    sib = dev(x, y, z, other)
    far = dev(x, wrap(y + 2, NY), z, core)
    far_sib = dev(x, wrap(y + 2, NY), z, other)
    n_ctx = 2 * NZ
    rp = {"dp": x, "context": wrap(r + 1, n_ctx), "tensor": t}
    rm = {"dp": x, "context": wrap(r - 1, n_ctx), "tensor": t}
    links = Links(send, recv)

    local = [
        pltpu.make_async_copy(w_out, wv.at[x, yl, z], loc.at[0]),
        pltpu.make_async_copy(w_query, qv.at[core, x, y, z], loc.at[1]),
        pltpu.make_async_copy(grad_out, tg.at[t], loc.at[2]),
        pltpu.make_async_copy(w_key, kvw.at[0:HD], loc.at[3]),
        pltpu.make_async_copy(w_value, kvw.at[HD : 2 * HD], loc.at[4]),
    ]
    for c in local:
        c.start()
    partners = (xp, xm, yp, ym, zp, zm, rp, rm, sib, far, far_sib)
    barrier = pltpu.get_barrier_semaphore()
    for d in partners:
        pl.semaphore_signal(barrier, inc=1, device_id=d, device_id_type=MESH)
    att_t[...] = attended[...].astype(F32).T.astype(BF)
    pl.semaphore_wait(barrier, len(partners))

    rows = 16
    n_pieces = 64 // rows
    sib_waits = []

    def grads_stream():
        first = []
        for k in range(n_pieces):
            a, b = pl.ds(k * rows, rows), pl.ds(64 + k * rows, rows)
            first.append(
                (
                    links.copy(grad_out.at[a], fwd.at[0, a], yp),
                    links.copy(grad_out.at[b], fwd.at[1, a], ym),
                )
            )
        sib_waits.append(links.copy(grad_out, tg.at[t], sib))
        yield
        second = []
        from_below = lax.div(wrap(y - 1, NY), 2) * 2 + core
        from_above = lax.div(wrap(y + 1, NY), 2) * 2 + core
        for k in range(n_pieces):
            a, b = pl.ds(k * rows, rows), pl.ds(64 + k * rows, rows)
            first[k][0].wait_recv()
            u = links.copy(fwd.at[0, a], tg.at[from_below, a], yp)
            first[k][1].wait_recv()
            second.append((u, links.copy(fwd.at[1, a], tg.at[from_above, b], ym)))
            yield
        for k in range(n_pieces):
            a, b = pl.ds(k * rows, rows), pl.ds(64 + k * rows, rows)
            second[k][0].wait_recv()
            sib_waits.append(links.copy(tg.at[partner, a], tg.at[partner, a], sib))
            second[k][1].wait_recv()
            sib_waits.append(links.copy(tg.at[partner, b], tg.at[partner, b], sib))
            yield
        for c in sib_waits:
            c.wait_recv()

    def w_out_stream(part):
        hs = pl.ds(64 * part, 64)
        c = links.copy(wv.at[x, yl, z, hs], wv.at[x, yl, z, hs], pair)
        yield
        c.wait_recv()
        if part == 0:
            yield from ring_gather(links, NX, x, lambda i: wv.at[i, :, z, hs], 1, xp, xm)
            yield from ring_gather(links, NZ, z, lambda i: wv.at[:, :, i, hs], 2, zp, zm)
        else:
            yield from ring_gather(links, NZ, z, lambda i: wv.at[x, :, i, hs], 1, zp, zm)
            yield from ring_gather(links, NX, x, lambda i: wv.at[i, :, :, hs], 1, xp, xm)

    q_waits = []

    def w_query_stream(part):
        hs = pl.ds(128 * part, 128)

        def hand_over(piece):
            q_waits.append(links.copy(piece, piece, sib))

        yield from ring_gather(links, NY, y, lambda i: qv.at[core, x, i, z, hs], 64, yp, ym)
        if part == 0:
            yield from ring_gather(links, NX, x, lambda i: qv.at[core, i, :, z, hs], 2, xp, xm)
            yield from ring_gather(
                links, NZ, z, lambda i: qv.at[core, :, :, i, hs], 2, zp, zm, hand_over
            )
        else:
            yield from ring_gather(links, NZ, z, lambda i: qv.at[core, x, :, i, hs], 2, zp, zm)
            yield from ring_gather(
                links, NX, x, lambda i: qv.at[core, i, :, :, hs], 2, xp, xm, hand_over
            )

    live = {}

    def go(*names):
        for name in names:
            if name in live:
                try:
                    next(live[name])
                except StopIteration:
                    del live[name]

    def finish(*names):
        while any(name in live for name in names):
            go(*names)

    local[0].wait()
    local[1].wait()
    live["wa"], live["wb"] = w_out_stream(0), w_out_stream(1)
    live["qa"], live["qb"] = w_query_stream(0), w_query_stream(1)
    live["g"] = grads_stream()
    go("wa", "wb", "qa", "qb", "g")
    halo_copies = [
        links.copy(keys.at[0:SPAN], halo.at[0, 0], rp),
        links.copy(values.at[0:SPAN], halo.at[0, 1], rp),
        links.copy(keys.at[SPAN : 2 * SPAN], halo.at[1, 0], rm),
        links.copy(values.at[SPAN : 2 * SPAN], halo.at[1, 1], rm),
    ]
    go("wa", "wb", "qa", "qb")
    go("wa", "wb")
    go("wa", "wb", "g", "qa", "qb")
    go("wa", "wb", "qa", "qb", "g")
    go("wa", "wb", "qb", "g")
    while "wa" in live or "wb" in live or "g" in live:
        go("wa", "wb", "g", "qb", "qa")
    for c in local[2:]:
        c.wait()
    for c in halo_copies:
        c.wait_recv()

    half_width = 4 * HD

    def dw_step(j, carry):
        at = pl.ds(pl.multiple_of(j * half_width, half_width), half_width)
        lhs = tg[:, :, at].reshape(2 * SPAN, half_width)
        part = jnp.dot(att_t[...], lhs, preferred_element_type=F32).astype(BF)
        xi, rest = lax.div(j, 4), lax.rem(j, 4)
        yi, zi = lax.div(rest, 2), lax.rem(rest, 2) * 4
        for q in range(4):
            pb[xi, yi, zi + q] = part[:, q * HD : (q + 1) * HD]
        return carry

    lax.fori_loop(0, 16, dw_step, 0)

    lo, hi = pl.ds(0, HD), pl.ds(HD, HD)

    def reduce_a():
        yield from ring_reduce(links, NZ, z, lambda i: pb.at[:, :, i, lo], raz, 2, zp, zm)
        yield from ring_reduce(links, NX, x, lambda i: pb.at[i, :, z, lo], rax, 1, xp, xm)
        c = links.copy(pb.at[x, 1 - yl, z, lo], ray, pair)
        yield
        c.wait_recv()
        total = pb[x, yl, z, lo].astype(F32) + ray[...].astype(F32)
        dwo[:, 0:HD] = total.T

    def reduce_b():
        yield from ring_reduce(links, NX, x, lambda i: pb.at[i, :, :, hi], rbx, 1, xp, xm)
        yield from ring_reduce(links, NZ, z, lambda i: pb.at[x, :, i, hi], rbz, 1, zp, zm)
        c = links.copy(pb.at[x, 1 - yl, z, hi], rby, pair)
        yield
        c.wait_recv()
        total = pb[x, yl, z, hi].astype(F32) + rby[...].astype(F32)
        dwo[:, HD : 2 * HD] = total.T

    live["ra"], live["rb"] = reduce_a(), reduce_b()
    go("ra", "rb")

    acc[...] = jnp.zeros_like(acc)

    def ag_step(j, carry):
        at = pl.ds(pl.multiple_of(j * half_width, half_width), half_width)
        lhs = tg[:, :, at].reshape(2 * SPAN, half_width)
        xi, rest = lax.div(j, 4), lax.rem(j, 4)
        yi, zi = lax.div(rest, 2), lax.rem(rest, 2) * 4
        rhs = wv[xi, yi, pl.ds(zi, 4)].reshape(half_width, 2 * HD)
        acc[...] += jnp.dot(lhs, rhs, preferred_element_type=F32)
        return carry

    lax.fori_loop(0, 16, ag_step, 0)
    ag[...] = acc[...].astype(BF)
    go("ra", "rb")

    last = r == n_ctx - 1
    inv_root = 1.0 / math.sqrt(HD)
    row_at = lax.broadcasted_iota(jnp.int32, (SPAN, SPAN), 0)
    col_at = lax.broadcasted_iota(jnp.int32, (SPAN, SPAN), 1)
    eye = row_at == col_at
    q_at = lax.broadcasted_iota(jnp.int32, (SPAN, 2 * SPAN), 0)
    k_at = lax.broadcasted_iota(jnp.int32, (SPAN, 2 * SPAN), 1) - SPAN

    def column(row, zero):
        return jnp.sum(jnp.where(eye, row, zero), axis=1, keepdims=True)

    def seg_of(span):
        return seg[:, pl.ds(pl.multiple_of(span * SPAN, SPAN), SPAN)]

    def unit(b, h):
        rows_b, cols_h = pl.ds(b * SPAN, SPAN), pl.ds(h * HD, HD)
        span = r if b == 0 else 2 * n_ctx - 1 - r
        seg_q = seg_of(span)
        seg_k = jnp.concatenate([seg_of(jnp.maximum(span - 1, 0)), seg_q], axis=1)
        allowed = (
            (k_at <= q_at)
            & (k_at + span * SPAN >= 0)
            & (seg_k == column(seg_q, 0))
        )
        prev_k, prev_v = halo[b, 0], halo[b, 1]
        if b == 1:
            prev_k = jnp.where(last, keys[0:SPAN], prev_k)
            prev_v = jnp.where(last, values[0:SPAN], prev_v)
        k_cat = jnp.concatenate([prev_k, keys[rows_b]], axis=0)
        v_cat = jnp.concatenate([prev_v, values[rows_b]], axis=0)
        qb, db = queries[rows_b, cols_h], ag[rows_b, cols_h]
        delta = jnp.sum(
            db.astype(F32) * attended[rows_b, cols_h].astype(F32), axis=1, keepdims=True
        )
        lse = column(log_sums[h : h + 1, rows_b], 0.0)
        scores = contract(qb, k_cat, 1, 1) * inv_root
        prob = jnp.where(allowed, jnp.exp(scores - lse), 0.0)
        dprob = contract(db, v_cat, 1, 1)
        dscore = (prob * (dprob - delta)).astype(BF)
        dq = jnp.dot(dscore, k_cat, preferred_element_type=F32) * inv_root
        qkv[rows_b, cols_h] = dq.astype(BF)
        kg = contract(dscore, qb, 0, 0) * inv_root
        vg = contract(prob.astype(BF), db, 0, 0)
        if h == 0:
            kvg[b, :, 0:HD] = kg
            kvg[b, :, HD : 2 * HD] = vg
        else:
            kvg[b, :, 0:HD] += kg
            kvg[b, :, HD : 2 * HD] += vg

    for b in range(2):
        for h in range(2):
            unit(b, h)
            go("ra", "rb")

    kvback[0] = kvg[0, 0:SPAN].astype(BF)
    kvback[1] = jnp.where(last, 0.0, kvg[1, 0:SPAN]).astype(BF)
    to_left = links.copy(kvback.at[0], kvland.at[0], rm)
    to_right = links.copy(kvback.at[1], kvland.at[1], rp)
    to_left.wait_recv()
    to_right.wait_recv()
    low = (
        kvg[0, SPAN : 2 * SPAN]
        + jnp.where(last, kvg[1, 0:SPAN], 0.0)
        + kvland[0].astype(F32)
    )
    high = kvg[1, SPAN : 2 * SPAN] + kvland[1].astype(F32)
    qkv[0:SPAN, 2 * HD : 4 * HD] = low.astype(BF)
    qkv[SPAN : 2 * SPAN, 2 * HD : 4 * HD] = high.astype(BF)

    def rows_of(d):
        return pl.ds(pl.multiple_of(d * HD, HD), HD)

    sib_t, far_sib_t = 2 * yh + other, 2 * (1 - yh) + other
    swaps = [
        links.copy(qkv.at[rows_of(partner)], ab.at[t], far),
        links.copy(qkv.at[rows_of(far_sib_t)], ab.at[t], far_sib),
        links.copy(qkv.at[rows_of(sib_t)], ab.at[t], sib),
    ]
    ab[t] = qkv[rows_of(t)]
    finish("ra", "rb")
    finish("qa", "qb")
    for c in swaps:
        c.wait_recv()
    for c in q_waits:
        c.wait_recv()

    kv_sum = jnp.sum(ab[:, :, 2 * HD : 4 * HD].astype(F32), axis=0).astype(BF)

    def out_step(j, carry):
        xi, yi = lax.div(j, 2), lax.rem(j, 2)
        for q in range(4):
            at = pl.ds(pl.multiple_of(j * (NZ * HD) + q * 2 * HD, 2 * HD), 2 * HD)
            total = jnp.dot(kv_sum, kvw[:, at], preferred_element_type=F32)
            for g in range(4):
                rhs = jnp.concatenate(
                    [
                        qv[g % 2, xi, 2 * (g // 2) + yi, 2 * q],
                        qv[g % 2, xi, 2 * (g // 2) + yi, 2 * q + 1],
                    ],
                    axis=1,
                )
                total += jnp.dot(ab[g, :, 0 : 2 * HD], rhs, preferred_element_type=F32)
            gin[:, at] = total.astype(BF)
        return carry

    lax.fori_loop(0, 8, out_step, 0)
    for c in links.started:
        c.wait_send()


def on_device(
    grad_out, queries, attended, keys, values, log_sums, segment_ids, w_out, w_query, w_key, w_value
):
    vmem = pl.BlockSpec(memory_space=pltpu.VMEM)
    hbm = pl.BlockSpec(memory_space=pl.ANY)
    own, model = grad_out.shape
    blocks = (NX, 2, NZ)
    return pl.pallas_call(
        kernel,
        out_shape=(
            jax.ShapeDtypeStruct((own, model), BF),
            jax.ShapeDtypeStruct((HD, 2 * HD), F32),
        ),
        in_specs=[hbm] + [vmem] * 6 + [hbm] * 4,
        out_specs=(vmem, vmem),
        scratch_shapes=[
            pltpu.VMEM((4, own, model), BF),
            pltpu.VMEM((2, 64, model), BF),
            pltpu.VMEM(blocks + (HD, 2 * HD), BF),
            pltpu.VMEM((2, NX, NY, NZ, 2 * HD, HD), BF),
            pltpu.VMEM((2 * HD, model), BF),
            pltpu.VMEM(blocks + (2 * HD, HD), BF),
            pltpu.VMEM((2, 4, NX, 2, HD, HD), BF),
            pltpu.VMEM((2, 2, 2, HD, HD), BF),
            pltpu.VMEM((HD, HD), BF),
            pltpu.VMEM((2, 2, 2, NZ, HD, HD), BF),
            pltpu.VMEM((2, 4, 2, HD, HD), BF),
            pltpu.VMEM((HD, HD), BF),
            pltpu.VMEM((2, 2, SPAN, HD), BF),
            pltpu.VMEM((2 * SPAN, 2 * HD), BF),
            pltpu.VMEM((2 * HD, 2 * SPAN), BF),
            pltpu.VMEM((2 * SPAN, 2 * HD), F32),
            pltpu.VMEM((2 * SPAN, 4 * HD), BF),
            pltpu.VMEM((2, 2 * SPAN, 2 * HD), F32),
            pltpu.VMEM((2, SPAN, 2 * HD), BF),
            pltpu.VMEM((2, SPAN, 2 * HD), BF),
            pltpu.VMEM((4, HD, 4 * HD), BF),
            pltpu.SemaphoreType.DMA((N_REMOTE,)),
            pltpu.SemaphoreType.DMA((N_REMOTE,)),
            pltpu.SemaphoreType.DMA((N_LOCAL,)),
        ],
        compiler_params=pltpu.CompilerParams(
            collective_id=0, has_side_effects=True, vmem_limit_bytes=60 * 2**20
        ),
    )(
        grad_out, queries, attended, keys, values, log_sums, segment_ids, w_out, w_query, w_key, w_value
    )


def solution(mesh):
    placed = (
        P(("dp", "context", "tensor"), None),
        P(("dp", "context"), "tensor"),
        P(("dp", "context"), "tensor"),
        P(("dp", "context"), None),
        P(("dp", "context"), None),
        P("tensor", ("dp", "context")),
        P("dp", None),
        P(("dp", "context"), "tensor"),
        P("tensor", ("dp", "context")),
        P(),
        P(),
    )
    return jax.shard_map(
        on_device,
        mesh=mesh,
        in_specs=placed,
        out_specs=(P(("dp", "context", "tensor"), None), P(("dp", "context"), "tensor")),
        check_vma=False,
    )
```

time: 1050 us -> 181 us (0.17)
  waiting for transfers between devices: 946 us -> 0 us
  Pallas kernels: 0 us -> 174 us
  matrix products: 58.6 us -> 0 us
  starting transfers between devices: 16.3 us -> 0 us
  between operations: 14 us -> 0.65 us
    all_gather x3 -> x0, waiting for transfers between devices: 539 us -> none  [the longest x1 262 us: on_device(): lax.all_gather(w_out, ('dp', 'context'), axis=0, tiled=True)]
    reduce_scatter x2 -> x0, waiting for transfers between devices: 396 us -> none  [the longest x1 301 us: on_device(): lax.psum_scatter(lax.dot_general(token_grads, attended, (((0,), (0,)), ((...]
    pallas_call x0 -> x1, Pallas kernels: none -> 174 us  [on_device(): pl.pallas_call(kernel, out_shape=(jax.ShapeDtypeStruct((own, model), BF),...]
    dot_general x10 -> x0, matrix products: 58.6 us -> none  [the longest x1 16.6 us: on_device(): jnp.dot(query_grads, query_full, preferred_element_type=jnp.float32)]
    ppermute x4 -> x0, starting transfers between devices: 16.2 us -> none  [the longest x2 12.3 us: extended_2(): after = lax.ppermute(initial, axis, down)]
  transfers between devices with their start and end apart: 9 -> 0, of which waited for: 7 -> 0; matrix products, arithmetic and copies ran while one was open for 6% -> 0% of each run, Pallas kernels for 0% -> 0%
where the time goes in v1:
time: 181 us; the launch traced here: 178 us
  Pallas kernels  174 us (96%)
  local copies, waits for them, and re-layouts  3.79 us (2%)
    pallas_call x1, Pallas kernels, on_device(): pl.pallas_call(kernel, out_shape=(jax.ShapeDtypeStruct((own, model), BF),...  174 us
    unnamed x4, local copies, waits for them, and re-layouts  3.79 us

profile of v1, /device:TPU:8, one launch (start us, length us, event | category | flops | bytes accessed | tf_op | source)
XLA Modules:
  0.0 178.2 jit_solution(172577075064530906)
XLA Ops:
  0.6 173.7 %shard_map.122 = (bf16[128,8192]{1,0:T(8,128)(2,1)}, f32[128,256]{1,0:T(8,128)}) custom-call(bf16[128,8192]{1,0:T(8,128)(2,1)} %grad_out.1, bf16[512,256]{1,0:T(8,128)(2,1)} %queries.1, bf16[512,256]{1,0:T(8,128)(2,1)} %attended.1, bf16[512,128]{1,0:T(8,128)(2,1)} %keys.1, bf16[512,128]{1,0:T(8,128)(2,1)} %values.1, f32[2,512]{1,0:T(2,128)} %log_sums.1, ...), custom_call_target="tpu_custom_call" | custom-call | tf_op jit(solution)/shard_map/pallas_call | solution.py:437
  174.4 0.0 copy-start
  174.4 3.1 %copy.15 = bf16[128,8192]{1,0:T(8,128)(2,1)} copy(bf16[128,8192]{1,0:T(8,128)(2,1)} %get-tuple-element.4) | data formatting | bytes 4194304
  177.5 0.0 copy-done
  177.5 0.7 copy.16
Async XLA Ops:
  174.4 3.1 %copy-start = (f32[128,256]{1,0:T(8,128)S(1)}, f32[128,256]{1,0:T(8,128)}, u32[]{:S(2)}) copy-start(f32[128,256]{1,0:T(8,128)} %get-tuple-element.5) | copy-start | bytes 393220

commit v2 on v1

v2 whole, which is shorter than its diff:
```python
import functools
import math

import jax
import jax.numpy as jnp
from jax import lax
from jax.experimental import pallas as pl
from jax.experimental.pallas import tpu as pltpu
from jax.sharding import PartitionSpec as P

MESH = pl.DeviceIdType.MESH
BF = jnp.bfloat16
F32 = jnp.float32
NX, NY, NZ = 4, 4, 8
SPAN = 256
HD = 128
N_REMOTE = 200
N_LOCAL = 8
WINDOW = 2
W_ROWS = 64
Q_ROWS = ((0, 48), (48, 96), (144, 112))
ORDER = (
    "gvwqrssqsrvwsqwsvrggvsgrsvwvrgggrgghabqr",
    "wahhbhqavhhhwhhcdsaqbcwbdvtttttcbaqrsabd",
    "btdcqrdsdcdtcypppyp",
)


def wrap(i, n):
    return lax.rem(i + n, n)


class Links:
    def __init__(self, send, recv):
        self.send, self.recv, self.started = send, recv, []

    def copy(self, src, dst, dev):
        n = len(self.started)
        c = pltpu.make_async_remote_copy(
            src_ref=src,
            dst_ref=dst,
            send_sem=self.send.at[n],
            recv_sem=self.recv.at[n],
            device_id=dev,
            device_id_type=MESH,
        )
        c.start()
        self.started.append(c)
        return c


def ring_gather(links, n, i, slab, half, up, down, arrived=None):
    k = n // 2
    cp = links.copy(slab(i), slab(i), up)
    cm = links.copy(slab(i), slab(i), down)
    if arrived is not None:
        arrived(slab(i))
    for s in range(1, k):
        yield
        before, after = slab(wrap(i - s, n)), slab(wrap(i + s, n))
        cp.wait_recv()
        piece = before if s < k - 1 or half is None else before.at[0:half]
        cp = links.copy(piece, piece, up)
        if arrived is not None:
            arrived(before)
        cm.wait_recv()
        if s < k - 1:
            cm = links.copy(after, after, down)
        elif half is not None:
            piece = after.at[half : 2 * half]
            cm = links.copy(piece, piece, down)
        else:
            cm = None
        if arrived is not None:
            arrived(after)
    yield
    cp.wait_recv()
    if cm is not None:
        cm.wait_recv()
    if arrived is not None:
        arrived(slab(wrap(i + k, n)))


def spread(links, piece, devs):
    copies = [links.copy(piece, piece, d) for d in devs]
    yield
    for c in copies:
        c.wait_recv()


def ring_reduce(links, n, i, slab, buf, half, up, down):
    k = n // 2
    far = wrap(i + k, n)
    cp = links.copy(slab(far).at[0:half], buf.at[0, 0, 0:half], up)
    cm = links.copy(slab(far).at[half : 2 * half], buf.at[1, 0, half : 2 * half], down)
    yield

    def add(dst, part):
        dst[...] = (dst[...].astype(F32) + part[...].astype(F32)).astype(BF)

    for step in range(1, k):
        s = k - step
        dst = slab(wrap(i + s, n))
        cp.wait_recv()
        if step == 1:
            add(dst.at[0:half], buf.at[0, 0, 0:half])
        else:
            add(dst, buf.at[0, step - 1])
        cp = links.copy(dst, buf.at[0, step], up)
        dst = slab(wrap(i - s, n))
        cm.wait_recv()
        if step == 1:
            add(dst.at[half : 2 * half], buf.at[1, 0, half : 2 * half])
        else:
            add(dst, buf.at[1, step - 1])
        cm = links.copy(dst, buf.at[1, step], down)
        yield
    cp.wait_recv()
    cm.wait_recv()
    dst = slab(i)
    dst[...] = (
        dst[...].astype(F32) + buf[0, k - 1].astype(F32) + buf[1, k - 1].astype(F32)
    ).astype(BF)


def spread_reduce(links, n, i, slab, buf, devs):
    copies = [
        links.copy(slab(wrap(i + step, n)), buf.at[j], d)
        for j, (step, d) in enumerate(zip((1, n - 1, 2), devs))
    ]
    yield
    for c in copies:
        c.wait_recv()
    dst = slab(i)
    total = dst[...].astype(F32)
    for j in range(3):
        total += buf[j].astype(F32)
    dst[...] = total.astype(BF)


def contract(a, b, da, db):
    return lax.dot_general(a, b, (((da,), (db,)), ((), ())), preferred_element_type=F32)


def kernel(
    grad_out, queries, attended, keys, values, log_sums, seg, w_out, w_query, w_key, w_value,
    gin, dwo,
    tg, wv, qv, kvw, pb, raz, rax, rbx, rbz, ry,
    halo, ag, att_t, acc, qkv, kvg, kvback, kvland, ab, send, recv, loc,
):
    x = lax.axis_index("dp")
    r = lax.axis_index("context")
    t = lax.axis_index("tensor")
    yl, z = lax.div(r, NZ), lax.rem(r, NZ)
    yh, core = lax.div(t, 2), lax.rem(t, 2)
    y = 2 * yh + yl
    other = 1 - core
    partner = 2 * (1 - yh) + core

    def dev(x, y, z, core):
        return {
            "dp": x,
            "context": lax.rem(y, 2) * NZ + z,
            "tensor": lax.div(y, 2) * 2 + core,
        }

    xp, xm = dev(wrap(x + 1, NX), y, z, core), dev(wrap(x - 1, NX), y, z, core)
    yp, ym = dev(x, wrap(y + 1, NY), z, core), dev(x, wrap(y - 1, NY), z, core)
    zp, zm = dev(x, y, wrap(z + 1, NZ), core), dev(x, y, wrap(z - 1, NZ), core)
    pair = dev(x, 2 * yh + 1 - yl, z, core)
    sib = dev(x, y, z, other)
    far = dev(x, wrap(y + 2, NY), z, core)
    far_x = dev(wrap(x + 2, NX), y, z, core)
    far_sib = dev(x, wrap(y + 2, NY), z, other)
    n_ctx = 2 * NZ
    rp = {"dp": x, "context": wrap(r + 1, n_ctx), "tensor": t}
    rm = {"dp": x, "context": wrap(r - 1, n_ctx), "tensor": t}
    links = Links(send, recv)

    local = [
        pltpu.make_async_copy(w_out, wv.at[x, yl, z], loc.at[0]),
        pltpu.make_async_copy(w_query, qv.at[core, x, y, z], loc.at[1]),
        pltpu.make_async_copy(grad_out, tg.at[t], loc.at[2]),
        pltpu.make_async_copy(w_key, kvw.at[0:HD], loc.at[3]),
        pltpu.make_async_copy(w_value, kvw.at[HD : 2 * HD], loc.at[4]),
    ]
    for c in local:
        c.start()
    partners = (xp, xm, yp, ym, zp, zm, rp, rm, sib, far, far_sib, far_x)
    barrier = pltpu.get_barrier_semaphore()
    for d in partners:
        pl.semaphore_signal(barrier, inc=1, device_id=d, device_id_type=MESH)
    att_t[...] = attended[...].astype(F32).T.astype(BF)
    pl.semaphore_wait(barrier, len(partners))

    halo_copies = [
        links.copy(keys.at[0:SPAN], halo.at[0, 0], rp),
        links.copy(values.at[0:SPAN], halo.at[0, 1], rp),
        links.copy(keys.at[SPAN : 2 * SPAN], halo.at[1, 0], rm),
        links.copy(values.at[SPAN : 2 * SPAN], halo.at[1, 1], rm),
    ]
    chunk = NZ * HD
    n_chunks = 2 * NX
    far_copies, own_copy, sib_copies = [], [], []

    def cols(j):
        return pl.ds(((j % NX) * 2 + j // NX) * chunk, chunk)

    def send_far():
        j = len(far_copies)
        if j < n_chunks:
            far_copies.append(links.copy(grad_out.at[:, cols(j)], tg.at[t, :, cols(j)], far))

    def dw_chunk(j):
        if j == 0:
            local[2].wait()
            own_copy[0].wait_recv()
        sib_copies[j].wait_recv()
        xi, yi = j % NX, j // NX

        def step(q, carry):
            at = pl.ds(pl.multiple_of((xi * 2 + yi) * chunk + q * 4 * HD, 4 * HD), 4 * HD)
            lhs = tg[:, :, at].reshape(2 * SPAN, 4 * HD)
            part = jnp.dot(att_t[...], lhs, preferred_element_type=F32).astype(BF)
            for u in range(4):
                pb[xi, yi, 4 * q + u] = part[:, u * HD : (u + 1) * HD]
            return carry

        lax.fori_loop(0, 2, step, 0)

    def grads_stream(first):
        yield
        if first == 0:
            for _ in range(WINDOW):
                send_far()
            own_copy.append(links.copy(grad_out, tg.at[t], sib))
        for j in range(first, first + NX):
            yield
            far_copies[j].wait_recv()
            send_far()
            got = tg.at[partner, :, cols(j)]
            sib_copies.append(links.copy(got, got, sib))
            if j > first:
                yield
                dw_chunk(j - 1)
        yield
        dw_chunk(first + NX - 1)

    def w_out_stream(part):
        hs = pl.ds(0, W_ROWS) if part == 0 else pl.ds(W_ROWS, HD - W_ROWS)
        yield
        c = links.copy(wv.at[x, yl, z, hs], wv.at[x, yl, z, hs], pair)
        yield
        c.wait_recv()
        if part == 0:
            yield from spread(links, wv.at[x, :, z, hs], (xp, xm, far_x))
            yield from ring_gather(links, NZ, z, lambda i: wv.at[:, :, i, hs], 2, zp, zm)
        else:
            yield from ring_gather(links, NZ, z, lambda i: wv.at[x, :, i, hs], 1, zp, zm)
            yield from ring_gather(links, NX, x, lambda i: wv.at[i, :, :, hs], 1, xp, xm)

    q_waits = []

    def w_query_stream(part):
        lo_row, n_rows = Q_ROWS[part]
        hs = pl.ds(lo_row, n_rows)

        def hand_over(piece):
            q_waits.append(links.copy(piece, piece, sib))

        yield
        if part == 2:
            yield from ring_gather(links, NZ, z, lambda i: qv.at[core, x, y, i, hs], None, zp, zm)
            yield from ring_gather(links, NX, x, lambda i: qv.at[core, i, y, :, hs], 4, xp, xm)
            yield
            yield from ring_gather(
                links, NY, y, lambda i: qv.at[core, :, i, :, hs], 2, yp, ym, hand_over
            )
            return
        yield from spread(links, qv.at[core, x, y, z, hs], (yp, ym, far))
        if part == 0:
            yield from spread(links, qv.at[core, x, :, z, hs], (xp, xm, far_x))
            yield
            yield from ring_gather(
                links, NZ, z, lambda i: qv.at[core, :, :, i, hs], 2, zp, zm, hand_over
            )
        else:
            yield from ring_gather(links, NZ, z, lambda i: qv.at[core, x, :, i, hs], 2, zp, zm)
            yield
            yield from ring_gather(
                links, NX, x, lambda i: qv.at[core, i, :, :, hs], 2, xp, xm, hand_over
            )

    lo, hi = pl.ds(0, HD), pl.ds(HD, HD)

    def reduce_a(yi):
        yield
        yield from ring_reduce(
            links, NZ, z, lambda i: pb.at[:, yi, i, lo], raz.at[yi], 2, zp, zm
        )
        yield from spread_reduce(
            links, NX, x, lambda i: pb.at[i, yi, z, lo], rax.at[yi], (xp, xm, far_x)
        )

    def reduce_b(yi):
        yield
        yield from ring_reduce(
            links, NX, x, lambda i: pb.at[i, yi, :, hi], rbx.at[yi], 4, xp, xm
        )
        yield from ring_reduce(
            links, NZ, z, lambda i: pb.at[x, yi, i, hi], rbz.at[yi], 64, zp, zm
        )

    def pair_sum():
        yield
        c = links.copy(pb.at[x, 1 - yl, z], ry, pair)
        yield
        c.wait_recv()
        dwo[...] = (pb[x, yl, z].astype(F32) + ry[...].astype(F32)).T

    def ag_steps(first):
        def step(j, carry):
            at = pl.ds(pl.multiple_of(j * 4 * HD, 4 * HD), 4 * HD)
            lhs = tg[:, :, at].reshape(2 * SPAN, 4 * HD)
            xi, rest = lax.div(j, 4), lax.rem(j, 4)
            yi, zi = lax.div(rest, 2), lax.rem(rest, 2) * 4
            rhs = wv[xi, yi, pl.ds(zi, 4)].reshape(4 * HD, 2 * HD)
            acc[...] += jnp.dot(lhs, rhs, preferred_element_type=F32)
            return carry

        lax.fori_loop(first, first + 4, step, 0)

    last = r == n_ctx - 1
    inv_root = 1.0 / math.sqrt(HD)
    row_at = lax.broadcasted_iota(jnp.int32, (SPAN, SPAN), 0)
    col_at = lax.broadcasted_iota(jnp.int32, (SPAN, SPAN), 1)
    eye = row_at == col_at
    q_at = lax.broadcasted_iota(jnp.int32, (SPAN, 2 * SPAN), 0)
    k_at = lax.broadcasted_iota(jnp.int32, (SPAN, 2 * SPAN), 1) - SPAN

    def column(row, zero):
        return jnp.sum(jnp.where(eye, row, zero), axis=1, keepdims=True)

    def seg_of(span):
        return seg[:, pl.ds(pl.multiple_of(span * SPAN, SPAN), SPAN)]

    def unit(b, h):
        rows_b, cols_h = pl.ds(b * SPAN, SPAN), pl.ds(h * HD, HD)
        span = r if b == 0 else 2 * n_ctx - 1 - r
        seg_q = seg_of(span)
        seg_k = jnp.concatenate([seg_of(jnp.maximum(span - 1, 0)), seg_q], axis=1)
        allowed = (
            (k_at <= q_at)
            & (k_at + span * SPAN >= 0)
            & (seg_k == column(seg_q, 0))
        )
        prev_k, prev_v = halo[b, 0], halo[b, 1]
        if b == 1:
            prev_k = jnp.where(last, keys[0:SPAN], prev_k)
            prev_v = jnp.where(last, values[0:SPAN], prev_v)
        k_cat = jnp.concatenate([prev_k, keys[rows_b]], axis=0)
        v_cat = jnp.concatenate([prev_v, values[rows_b]], axis=0)
        qb, db = queries[rows_b, cols_h], ag[rows_b, cols_h]
        delta = jnp.sum(
            db.astype(F32) * attended[rows_b, cols_h].astype(F32), axis=1, keepdims=True
        )
        lse = column(log_sums[h : h + 1, rows_b], 0.0)
        scores = contract(qb, k_cat, 1, 1) * inv_root
        prob = jnp.where(allowed, jnp.exp(scores - lse), 0.0)
        dprob = contract(db, v_cat, 1, 1)
        dscore = (prob * (dprob - delta)).astype(BF)
        dq = jnp.dot(dscore, k_cat, preferred_element_type=F32) * inv_root
        qkv[rows_b, cols_h] = dq.astype(BF)
        kg = contract(dscore, qb, 0, 0) * inv_root
        vg = contract(prob.astype(BF), db, 0, 0)
        if h == 0:
            kvg[b, :, 0:HD] = kg
            kvg[b, :, HD : 2 * HD] = vg
        else:
            kvg[b, :, 0:HD] += kg
            kvg[b, :, HD : 2 * HD] += vg

    def rows_of(d):
        return pl.ds(pl.multiple_of(d * HD, HD), HD)

    def attention_stream():
        for part in range(4):
            yield
            if part == 0:
                acc[...] = jnp.zeros_like(acc)
            ag_steps(4 * part)
        yield
        ag[...] = acc[...].astype(BF)
        for c in halo_copies:
            c.wait_recv()
        for b in range(2):
            for h in range(2):
                unit(b, h)
        kvback[0] = kvg[0, 0:SPAN].astype(BF)
        kvback[1] = jnp.where(last, 0.0, kvg[1, 0:SPAN]).astype(BF)
        to_left = links.copy(kvback.at[0], kvland.at[0], rm)
        to_right = links.copy(kvback.at[1], kvland.at[1], rp)
        yield
        to_left.wait_recv()
        to_right.wait_recv()
        low = (
            kvg[0, SPAN : 2 * SPAN]
            + jnp.where(last, kvg[1, 0:SPAN], 0.0)
            + kvland[0].astype(F32)
        )
        high = kvg[1, SPAN : 2 * SPAN] + kvland[1].astype(F32)
        qkv[0:SPAN, 2 * HD : 4 * HD] = low.astype(BF)
        qkv[SPAN : 2 * SPAN, 2 * HD : 4 * HD] = high.astype(BF)
        swaps = [
            links.copy(qkv.at[rows_of(partner)], ab.at[t], far),
            links.copy(qkv.at[rows_of(2 * (1 - yh) + other)], ab.at[t], far_sib),
            links.copy(qkv.at[rows_of(2 * yh + other)], ab.at[t], sib),
        ]
        ab[t] = qkv[rows_of(t)]
        yield
        for c in swaps:
            c.wait_recv()

    def out_stream():
        yield
        local[3].wait()
        local[4].wait()
        for c in q_waits:
            c.wait_recv()
        kv_sum = jnp.sum(ab[:, :, 2 * HD : 4 * HD].astype(F32), axis=0).astype(BF)

        def step(j, carry):
            xi, yi = lax.div(j, 2), lax.rem(j, 2)
            for q in range(4):
                at = pl.ds(pl.multiple_of(j * chunk + q * 2 * HD, 2 * HD), 2 * HD)
                total = jnp.dot(kv_sum, kvw[:, at], preferred_element_type=F32)
                for g in range(4):
                    heads = qv.at[g % 2, xi, 2 * (g // 2) + yi]
                    rhs = jnp.concatenate([heads[2 * q], heads[2 * q + 1]], axis=1)
                    total += jnp.dot(ab[g, :, 0 : 2 * HD], rhs, preferred_element_type=F32)
                gin[:, at] = total.astype(BF)
            return carry

        for part in range(4):
            lax.fori_loop(2 * part, 2 * part + 2, step, 0)
            if part < 3:
                yield

    local[0].wait()
    local[1].wait()
    live = {
        "w": w_out_stream(0),
        "v": w_out_stream(1),
        "g": grads_stream(0),
        "h": grads_stream(NX),
        "q": w_query_stream(0),
        "r": w_query_stream(1),
        "s": w_query_stream(2),
        "a": reduce_a(0),
        "b": reduce_b(0),
        "c": reduce_a(1),
        "d": reduce_b(1),
        "y": pair_sum(),
        "t": attention_stream(),
        "p": out_stream(),
    }
    for stream in live.values():
        next(stream)
    for name in "".join(ORDER):
        next(live[name], 0)
    for stream in live.values():
        assert next(stream, 0) == 0
    for c in links.started:
        c.wait_send()


def on_device(
    grad_out, queries, attended, keys, values, log_sums, segment_ids, w_out, w_query, w_key, w_value
):
    vmem = pl.BlockSpec(memory_space=pltpu.VMEM)
    hbm = pl.BlockSpec(memory_space=pl.ANY)
    own, model = grad_out.shape
    blocks = (NX, 2, NZ)
    return pl.pallas_call(
        kernel,
        out_shape=(
            jax.ShapeDtypeStruct((own, model), BF),
            jax.ShapeDtypeStruct((HD, 2 * HD), F32),
        ),
        in_specs=[hbm] + [vmem] * 6 + [hbm] * 4,
        out_specs=(vmem, vmem),
        scratch_shapes=[
            pltpu.VMEM((4, own, model), BF),
            pltpu.VMEM(blocks + (HD, 2 * HD), BF),
            pltpu.VMEM((2, NX, NY, NZ, 2 * HD, HD), BF),
            pltpu.VMEM((2 * HD, model), BF),
            pltpu.VMEM(blocks + (2 * HD, HD), BF),
            pltpu.VMEM((2, 2, 4, NX, HD, HD), BF),
            pltpu.VMEM((2, 3, HD, HD), BF),
            pltpu.VMEM((2, 2, 2, NZ, HD, HD), BF),
            pltpu.VMEM((2, 2, 4, HD, HD), BF),
            pltpu.VMEM((2 * HD, HD), BF),
            pltpu.VMEM((2, 2, SPAN, HD), BF),
            pltpu.VMEM((2 * SPAN, 2 * HD), BF),
            pltpu.VMEM((2 * HD, 2 * SPAN), BF),
            pltpu.VMEM((2 * SPAN, 2 * HD), F32),
            pltpu.VMEM((2 * SPAN, 4 * HD), BF),
            pltpu.VMEM((2, 2 * SPAN, 2 * HD), F32),
            pltpu.VMEM((2, SPAN, 2 * HD), BF),
            pltpu.VMEM((2, SPAN, 2 * HD), BF),
            pltpu.VMEM((4, HD, 4 * HD), BF),
            pltpu.SemaphoreType.DMA((N_REMOTE,)),
            pltpu.SemaphoreType.DMA((N_REMOTE,)),
            pltpu.SemaphoreType.DMA((N_LOCAL,)),
        ],
        compiler_params=pltpu.CompilerParams(
            collective_id=0, has_side_effects=True, vmem_limit_bytes=52 * 2**20
        ),
    )(
        grad_out, queries, attended, keys, values, log_sums, segment_ids, w_out, w_query, w_key, w_value
    )


def solution(mesh):
    placed = (
        P(("dp", "context", "tensor"), None),
        P(("dp", "context"), "tensor"),
        P(("dp", "context"), "tensor"),
        P(("dp", "context"), None),
        P(("dp", "context"), None),
        P("tensor", ("dp", "context")),
        P("dp", None),
        P(("dp", "context"), "tensor"),
        P("tensor", ("dp", "context")),
        P(),
        P(),
    )
    return jax.shard_map(
        on_device,
        mesh=mesh,
        in_specs=placed,
        out_specs=(P(("dp", "context", "tensor"), None), P(("dp", "context"), "tensor")),
        check_vma=False,
    )
```

time: 181 us -> 149 us (0.82)
  Pallas kernels: 174 us -> 136 us
  local copies, waits for them, and re-layouts: 3.79 us -> 10.6 us
    pallas_call x1, Pallas kernels: 174 us -> 136 us  [on_device(): pl.pallas_call(kernel, out_shape=(jax.ShapeDtypeStruct((own, model), BF),...]
    unnamed x4 -> x18, local copies, waits for them, and re-layouts: 3.79 us -> 10.6 us
where the time goes in v2:
time: 149 us; the launch traced here: 147 us
  Pallas kernels  136 us (91%)
  local copies, waits for them, and re-layouts  10.6 us (7%)
    pallas_call x1, Pallas kernels, on_device(): pl.pallas_call(kernel, out_shape=(jax.ShapeDtypeStruct((own, model), BF),...  136 us
    unnamed x18, local copies, waits for them, and re-layouts  10.6 us

profile of v2, /device:TPU:8, one launch (start us, length us, event | category | flops | bytes accessed | tf_op | source)
XLA Modules:
  0.0 147.4 jit_solution(1154500587516589357)
XLA Ops:
  0.6 0.0 copy-start
  0.6 0.9 copy-done
  1.6 0.0 copy-start.1
  1.6 0.9 copy-done.1
  2.5 0.0 copy-start.2
  2.5 0.9 copy-done.2
  3.4 0.0 copy-start.3
  3.4 0.9 copy-done.3
  4.3 0.0 copy-start.4
  4.3 0.8 copy-done.4
  5.2 0.0 copy-start.5
  5.2 0.8 copy-done.5
  6.0 0.0 copy-start.6
  6.0 0.8 copy-done.6
  6.8 0.0 copy-start.7
  6.8 0.7 copy-done.7
  7.5 136.2 %shard_map.122 = (bf16[128,8192]{1,0:T(8,128)(2,1)}, f32[128,256]{1,0:T(8,128)S(1)}) custom-call(bf16[128,8192]{1,0:T(8,128)(2,1)} %grad_out.1, bf16[512,256]{1,0:T(8,128)(2,1)S(1)} %copy-done, bf16[512,256]{1,0:T(8,128)(2,1)S(1)} %copy-done.1, bf16[512,128]{1,0:T(8,128)(2,1)S(1)} %copy-done.2, bf16[512,128]{1,0:T(8,128)(2,1)S(1)} %copy-done.3, ...), custom_call_target="tpu_custom_call" | custom-call | tf_op jit(solution)/shard_map/pallas_call | solution.py:484
  143.6 3.1 %copy.15 = bf16[128,8192]{1,0:T(8,128)(2,1)} copy(bf16[128,8192]{1,0:T(8,128)(2,1)} %get-tuple-element.4) | data formatting | bytes 4194304
  146.7 0.7 copy.16
Async XLA Ops:
  0.6 1.0 copy-start
  1.6 0.9 copy-start.1
  2.5 0.9 copy-start.2
  3.4 0.9 copy-start.3
  4.3 0.8 copy-start.4
  5.2 0.8 copy-start.5
  6.0 0.8 copy-start.6
  6.8 0.7 copy-start.7

commit v3 on v2

--- a/solution.py
+++ b/solution.py
@@ -16,13 +16,13 @@
 HD = 128
 N_REMOTE = 200
 N_LOCAL = 8
-WINDOW = 2
+WINDOW = 8
 W_ROWS = 64
-Q_ROWS = ((0, 48), (48, 96), (144, 112))
+Q_ROWS = ((0, 48), (48, 112), (160, 96))
 ORDER = (
-    "gvwqrssqsrvwsqwsvrggvsgrsvwvrgggrgghabqr",
-    "wahhbhqavhhhwhhcdsaqbcwbdvtttttcbaqrsabd",
-    "btdcqrdsdcdtcypppyp",
+    "svqrwgvswvssvqgrsvwvrsgwqggrggggbavhwbrs",
+    "qswhhrrqhhvhwabhhtqhtcbatttqcdsdbtarcqdd",
+    "casdbcrdtbacdyppppy",
 )
 
 
@@ -514,7 +514,7 @@
             pltpu.SemaphoreType.DMA((N_LOCAL,)),
         ],
         compiler_params=pltpu.CompilerParams(
-            collective_id=0, has_side_effects=True, vmem_limit_bytes=52 * 2**20
+            collective_id=0, has_side_effects=True, vmem_limit_bytes=60 * 2**20
         ),
     )(
         grad_out, queries, attended, keys, values, log_sums, segment_ids, w_out, w_query, w_key, w_value

time: 149 us -> 119 us (0.80)
  Pallas kernels: 136 us -> 114 us
  local copies, waits for them, and re-layouts: 10.6 us -> 3.79 us
    pallas_call x1, Pallas kernels: 136 us -> 114 us  [on_device(): pl.pallas_call(kernel, out_shape=(jax.ShapeDtypeStruct((own, model), BF),...]
    unnamed x18 -> x4, local copies, waits for them, and re-layouts: 10.6 us -> 3.79 us
where the time goes in v3:
time: 119 us; the launch traced here: 118 us
  Pallas kernels  114 us (96%)
  local copies, waits for them, and re-layouts  3.79 us (3%)
    pallas_call x1, Pallas kernels, on_device(): pl.pallas_call(kernel, out_shape=(jax.ShapeDtypeStruct((own, model), BF),...  114 us
    unnamed x4, local copies, waits for them, and re-layouts  3.79 us

profile of v3, /device:TPU:8, one launch (start us, length us, event | category | flops | bytes accessed | tf_op | source)
XLA Modules:
  0.0 118.4 jit_solution(3636647123105222717)
XLA Ops:
  0.6 114.0 %shard_map.122 = (bf16[128,8192]{1,0:T(8,128)(2,1)}, f32[128,256]{1,0:T(8,128)}) custom-call(bf16[128,8192]{1,0:T(8,128)(2,1)} %grad_out.1, bf16[512,256]{1,0:T(8,128)(2,1)} %queries.1, bf16[512,256]{1,0:T(8,128)(2,1)} %attended.1, bf16[512,128]{1,0:T(8,128)(2,1)} %keys.1, bf16[512,128]{1,0:T(8,128)(2,1)} %values.1, f32[2,512]{1,0:T(2,128)} %log_sums.1, ...), custom_call_target="tpu_custom_call" | custom-call | tf_op jit(solution)/shard_map/pallas_call | solution.py:484
  114.6 0.0 copy-start
  114.7 3.1 %copy.15 = bf16[128,8192]{1,0:T(8,128)(2,1)} copy(bf16[128,8192]{1,0:T(8,128)(2,1)} %get-tuple-element.4) | data formatting | bytes 4194304
  117.8 0.0 copy-done
  117.8 0.7 copy.16
Async XLA Ops:
  114.6 3.1 %copy-start = (f32[128,256]{1,0:T(8,128)S(1)}, f32[128,256]{1,0:T(8,128)}, u32[]{:S(2)}) copy-start(f32[128,256]{1,0:T(8,128)} %get-tuple-element.5) | copy-start | bytes 393220

commit v4 on v3

--- a/solution.py
+++ b/solution.py
@@ -14,15 +14,15 @@
 NX, NY, NZ = 4, 4, 8
 SPAN = 256
 HD = 128
-N_REMOTE = 200
-N_LOCAL = 8
+N_REMOTE = 256
+N_LOCAL = 16
 WINDOW = 8
 W_ROWS = 64
-Q_ROWS = ((0, 48), (48, 112), (160, 96))
+Q_ROWS = ((0, 64), (64, 96), (160, 96))
 ORDER = (
-    "svqrwgvswvssvqgrsvwvrsgwqggrggggbavhwbrs",
-    "qswhhrrqhhvhwabhhtqhtcbatttqcdsdbtarcqdd",
-    "casdbcrdtbacdyppppy",
+    "swvrqwgvsrvqswvsrqqsgrggwgggVvqVsggbvVwR",
+    "hhhqbVshhrswRVhhbahhcdbwqrcRaVbtdtRcttas",
+    "tRqdaRtdcdbsacdtabpcdypppy",
 )
 
 
@@ -81,8 +81,62 @@
         arrived(slab(wrap(i + k, n)))
 
 
-def spread(links, piece, devs):
-    copies = [links.copy(piece, piece, d) for d in devs]
+def pipelined_gather(links, z, x, slab, half, z_devs, x_devs):
+    zk = NZ // 2
+    sent = []
+
+    def along_x(zs):
+        ups, downs = [], []
+        for zi in zs:
+            piece = slab(x, zi)
+            ups.append(links.copy(piece, piece, x_devs[0]))
+            downs.append(links.copy(piece, piece, x_devs[1]))
+        sent.append((zs, ups, downs))
+
+    def first():
+        own = slab(x, z)
+        cp, cm = links.copy(own, own, z_devs[0]), links.copy(own, own, z_devs[1])
+        along_x((z,))
+        for s in range(1, zk):
+            yield
+            before, after = wrap(z - s, NZ), wrap(z + s, NZ)
+            cp.wait_recv()
+            cm.wait_recv()
+            up, down = slab(x, before), slab(x, after)
+            if s == zk - 1:
+                up, down = up.at[0:half], down.at[half : 2 * half]
+            cp, cm = links.copy(up, up, z_devs[0]), links.copy(down, down, z_devs[1])
+            along_x((before, after))
+        yield
+        cp.wait_recv()
+        cm.wait_recv()
+        along_x((wrap(z + zk, NZ),))
+
+    def second():
+        before, after = wrap(x - 1, NX), wrap(x + 1, NX)
+        halves = []
+        for k in range(zk + 1):
+            yield
+            zs, ups, downs = sent[k]
+            for zi, up, down in zip(zs, ups, downs):
+                up.wait_recv()
+                down.wait_recv()
+                got = slab(before, zi)
+                piece = got.at[0:half]
+                halves.append(links.copy(piece, piece, x_devs[0]))
+                got = slab(after, zi)
+                piece = got.at[half : 2 * half]
+                halves.append(links.copy(piece, piece, x_devs[1]))
+        yield
+        for c in halves:
+            c.wait_recv()
+
+    return first, second
+
+
+def spread(links, piece, devs, source=None):
+    source = piece if source is None else source
+    copies = [links.copy(source, piece, d) for d in devs]
     yield
     for c in copies:
         c.wait_recv()
@@ -143,9 +197,10 @@
 
 
 def kernel(
-    grad_out, queries, attended, keys, values, log_sums, seg, w_out, w_query, w_key, w_value,
-    gin, dwo,
-    tg, wv, qv, kvw, pb, raz, rax, rbx, rbz, ry,
+    grad_out, queries_in, attended_in, keys_in, values_in, log_sums_in, seg_in,
+    w_out, w_query, w_key, w_value,
+    gin_out, dwo,
+    queries, attended, keys, values, log_sums, seg, gin, tg, wv, qv, kvw, pb, raz, rax, rbx, rbz, ry,
     halo, ag, att_t, acc, qkv, kvg, kvback, kvland, ab, send, recv, loc,
 ):
     x = lax.axis_index("dp")
@@ -183,25 +238,25 @@
         pltpu.make_async_copy(grad_out, tg.at[t], loc.at[2]),
         pltpu.make_async_copy(w_key, kvw.at[0:HD], loc.at[3]),
         pltpu.make_async_copy(w_value, kvw.at[HD : 2 * HD], loc.at[4]),
+        pltpu.make_async_copy(attended_in, attended, loc.at[5]),
+        pltpu.make_async_copy(queries_in, queries, loc.at[6]),
+        pltpu.make_async_copy(keys_in, keys, loc.at[7]),
+        pltpu.make_async_copy(values_in, values, loc.at[8]),
+        pltpu.make_async_copy(log_sums_in, log_sums, loc.at[9]),
+        pltpu.make_async_copy(seg_in, seg, loc.at[10]),
     ]
-    for c in local:
-        c.start()
     partners = (xp, xm, yp, ym, zp, zm, rp, rm, sib, far, far_sib, far_x)
     barrier = pltpu.get_barrier_semaphore()
     for d in partners:
         pl.semaphore_signal(barrier, inc=1, device_id=d, device_id_type=MESH)
-    att_t[...] = attended[...].astype(F32).T.astype(BF)
+    for c in local:
+        c.start()
     pl.semaphore_wait(barrier, len(partners))
 
-    halo_copies = [
-        links.copy(keys.at[0:SPAN], halo.at[0, 0], rp),
-        links.copy(values.at[0:SPAN], halo.at[0, 1], rp),
-        links.copy(keys.at[SPAN : 2 * SPAN], halo.at[1, 0], rm),
-        links.copy(values.at[SPAN : 2 * SPAN], halo.at[1, 1], rm),
-    ]
     chunk = NZ * HD
     n_chunks = 2 * NX
-    far_copies, own_copy, sib_copies = [], [], []
+    ready = set()
+    far_copies, own_copy, sib_copies, halo_copies = [], [], [], []
 
     def cols(j):
         return pl.ds(((j % NX) * 2 + j // NX) * chunk, chunk)
@@ -249,16 +304,22 @@
     def w_out_stream(part):
         hs = pl.ds(0, W_ROWS) if part == 0 else pl.ds(W_ROWS, HD - W_ROWS)
         yield
-        c = links.copy(wv.at[x, yl, z, hs], wv.at[x, yl, z, hs], pair)
-        yield
+        c = links.copy(w_out.at[hs], wv.at[x, yl, z, hs], pair)
+        yield
+        if 0 not in ready:
+            local[0].wait()
+            ready.add(0)
         c.wait_recv()
         if part == 0:
             yield from spread(links, wv.at[x, :, z, hs], (xp, xm, far_x))
             yield from ring_gather(links, NZ, z, lambda i: wv.at[:, :, i, hs], 2, zp, zm)
         else:
-            yield from ring_gather(links, NZ, z, lambda i: wv.at[x, :, i, hs], 1, zp, zm)
-            yield from ring_gather(links, NX, x, lambda i: wv.at[i, :, :, hs], 1, xp, xm)
-
+            yield from w_first()
+
+    w_rest = pl.ds(W_ROWS, HD - W_ROWS)
+    w_first, w_second = pipelined_gather(
+        links, z, x, lambda i, j: wv.at[i, :, j, w_rest], 1, (zp, zm), (xp, xm)
+    )
     q_waits = []
 
     def w_query_stream(part):
@@ -270,6 +331,9 @@
 
         yield
         if part == 2:
+            if 1 not in ready:
+                local[1].wait()
+                ready.add(1)
             yield from ring_gather(links, NZ, z, lambda i: qv.at[core, x, y, i, hs], None, zp, zm)
             yield from ring_gather(links, NX, x, lambda i: qv.at[core, i, y, :, hs], 4, xp, xm)
             yield
@@ -277,7 +341,10 @@
                 links, NY, y, lambda i: qv.at[core, :, i, :, hs], 2, yp, ym, hand_over
             )
             return
-        yield from spread(links, qv.at[core, x, y, z, hs], (yp, ym, far))
+        yield from spread(links, qv.at[core, x, y, z, hs], (yp, ym, far), w_query.at[hs])
+        if 1 not in ready:
+            local[1].wait()
+            ready.add(1)
         if part == 0:
             yield from spread(links, qv.at[core, x, :, z, hs], (xp, xm, far_x))
             yield
@@ -285,11 +352,18 @@
                 links, NZ, z, lambda i: qv.at[core, :, :, i, hs], 2, zp, zm, hand_over
             )
         else:
-            yield from ring_gather(links, NZ, z, lambda i: qv.at[core, x, :, i, hs], 2, zp, zm)
-            yield
-            yield from ring_gather(
-                links, NX, x, lambda i: qv.at[core, i, :, :, hs], 2, xp, xm, hand_over
-            )
+            yield from q_first()
+
+    q_rest = pl.ds(Q_ROWS[1][0], Q_ROWS[1][1])
+    q_first, q_second = pipelined_gather(
+        links, z, x, lambda i, j: qv.at[core, i, :, j, q_rest], 2, (zp, zm), (xp, xm)
+    )
+
+    def q_tail():
+        yield from q_second()
+        for i in range(NX):
+            piece = qv.at[core, i, :, :, q_rest]
+            q_waits.append(links.copy(piece, piece, sib))
 
     lo, hi = pl.ds(0, HD), pl.ds(HD, HD)
 
@@ -391,6 +465,8 @@
             ag_steps(4 * part)
         yield
         ag[...] = acc[...].astype(BF)
+        for c in local[6:]:
+            c.wait()
         for c in halo_copies:
             c.wait_recv()
         for b in range(2):
@@ -420,6 +496,8 @@
         yield
         for c in swaps:
             c.wait_recv()
+
+    out_copies = []
 
     def out_stream():
         yield
@@ -443,11 +521,12 @@
 
         for part in range(4):
             lax.fori_loop(2 * part, 2 * part + 2, step, 0)
+            at = pl.ds(2 * part * chunk, 2 * chunk)
+            out_copies.append(pltpu.make_async_copy(gin.at[:, at], gin_out.at[:, at], loc.at[11 + part]))
+            out_copies[-1].start()
             if part < 3:
                 yield
 
-    local[0].wait()
-    local[1].wait()
     live = {
         "w": w_out_stream(0),
         "v": w_out_stream(1),
@@ -463,15 +542,28 @@
         "y": pair_sum(),
         "t": attention_stream(),
         "p": out_stream(),
+        "V": w_second(),
+        "R": q_tail(),
     }
     for stream in live.values():
         next(stream)
-    for name in "".join(ORDER):
+    for n, name in enumerate("".join(ORDER)):
         next(live[name], 0)
+        if n == 5:
+            halo_copies.extend([
+                links.copy(keys_in.at[0:SPAN], halo.at[0, 0], rp),
+                links.copy(values_in.at[0:SPAN], halo.at[0, 1], rp),
+                links.copy(keys_in.at[SPAN : 2 * SPAN], halo.at[1, 0], rm),
+                links.copy(values_in.at[SPAN : 2 * SPAN], halo.at[1, 1], rm),
+            ])
+            local[5].wait()
+            att_t[...] = attended[...].astype(F32).T.astype(BF)
     for stream in live.values():
         assert next(stream, 0) == 0
     for c in links.started:
         c.wait_send()
+    for c in out_copies:
+        c.wait()
 
 
 def on_device(
@@ -487,9 +579,16 @@
             jax.ShapeDtypeStruct((own, model), BF),
             jax.ShapeDtypeStruct((HD, 2 * HD), F32),
         ),
-        in_specs=[hbm] + [vmem] * 6 + [hbm] * 4,
-        out_specs=(vmem, vmem),
+        in_specs=[hbm] * 11,
+        out_specs=(hbm, vmem),
         scratch_shapes=[
+            pltpu.VMEM(queries.shape, BF),
+            pltpu.VMEM(attended.shape, BF),
+            pltpu.VMEM(keys.shape, BF),
+            pltpu.VMEM(values.shape, BF),
+            pltpu.VMEM(log_sums.shape, F32),
+            pltpu.VMEM(segment_ids.shape, jnp.int32),
+            pltpu.VMEM((own, model), BF),
             pltpu.VMEM((4, own, model), BF),
             pltpu.VMEM(blocks + (HD, 2 * HD), BF),
             pltpu.VMEM((2, NX, NY, NZ, 2 * HD, HD), BF),

time: 119 us -> 114 us (0.958)
  Pallas kernels: 114 us -> 109 us
    pallas_call x1, Pallas kernels: 114 us -> 109 us  [on_device(): pl.pallas_call(kernel, out_shape=(jax.ShapeDtypeStruct((own, model), BF),...]
where the time goes in v4:
time: 114 us
  Pallas kernels  109 us (96%)
  local copies, waits for them, and re-layouts  3.79 us (3%)
    pallas_call x1, Pallas kernels, on_device(): pl.pallas_call(kernel, out_shape=(jax.ShapeDtypeStruct((own, model), BF),...  109 us
    unnamed x4, local copies, waits for them, and re-layouts  3.79 us

profile of v4, /device:TPU:8, one launch (start us, length us, event | category | flops | bytes accessed | tf_op | source)
XLA Modules:
  0.0 113.7 jit_solution(10284447627062077489)
XLA Ops:
  0.6 109.2 %shard_map.122 = (bf16[128,8192]{1,0:T(8,128)(2,1)}, f32[128,256]{1,0:T(8,128)}) custom-call(bf16[128,8192]{1,0:T(8,128)(2,1)} %grad_out.1, bf16[512,256]{1,0:T(8,128)(2,1)} %queries_in.1, bf16[512,256]{1,0:T(8,128)(2,1)} %attended_in.1, bf16[512,128]{1,0:T(8,128)(2,1)} %keys_in.1, bf16[512,128]{1,0:T(8,128)(2,1)} %values_in.1, f32[2,512]{1,0:T(2,128)} %log_sums_in.1, ...), custom_call_target="tpu_custom_call" | custom-call | tf_op jit(solution)/shard_map/pallas_call | solution.py:576
  109.9 0.0 copy-start
  109.9 3.1 %copy.15 = bf16[128,8192]{1,0:T(8,128)(2,1)} copy(bf16[128,8192]{1,0:T(8,128)(2,1)} %get-tuple-element.4) | data formatting | bytes 4194304
  113.0 0.0 copy-done
  113.0 0.7 copy.16
Async XLA Ops:
  109.9 3.1 %copy-start = (f32[128,256]{1,0:T(8,128)S(1)}, f32[128,256]{1,0:T(8,128)}, u32[]{:S(2)}) copy-start(f32[128,256]{1,0:T(8,128)} %get-tuple-element.5) | copy-start | bytes 393220

commit v5 on v4

--- a/solution.py
+++ b/solution.py
@@ -566,6 +566,24 @@
         c.wait()
 
 
+N_OUT = 4
+
+
+def hand_out(gin, dwo, gin_out, dwo_out, gin_here, dwo_here, sems):
+    rows = gin.shape[0] // N_OUT
+    parts = [(gin.at[at], gin_here.at[at], gin_out.at[at]) for at in (pl.ds(k * rows, rows) for k in range(N_OUT))]
+    parts.append((dwo, dwo_here, dwo_out))
+    loads = [pltpu.make_async_copy(a, b, sems.at[0, k]) for k, (a, b, _) in enumerate(parts)]
+    stores = [pltpu.make_async_copy(b, c, sems.at[1, k]) for k, (_, b, c) in enumerate(parts)]
+    for c in loads:
+        c.start()
+    for load, store in zip(loads, stores):
+        load.wait()
+        store.start()
+    for c in stores:
+        c.wait()
+
+
 def on_device(
     grad_out, queries, attended, keys, values, log_sums, segment_ids, w_out, w_query, w_key, w_value
 ):
@@ -573,7 +591,7 @@
     hbm = pl.BlockSpec(memory_space=pl.ANY)
     own, model = grad_out.shape
     blocks = (NX, 2, NZ)
-    return pl.pallas_call(
+    results = pl.pallas_call(
         kernel,
         out_shape=(
             jax.ShapeDtypeStruct((own, model), BF),
@@ -618,6 +636,21 @@
     )(
         grad_out, queries, attended, keys, values, log_sums, segment_ids, w_out, w_query, w_key, w_value
     )
+    return pl.pallas_call(
+        hand_out,
+        out_shape=(
+            jax.ShapeDtypeStruct((own, model), BF),
+            jax.ShapeDtypeStruct((HD, 2 * HD), F32),
+        ),
+        in_specs=[hbm, hbm],
+        out_specs=(hbm, hbm),
+        scratch_shapes=[
+            pltpu.VMEM((own, model), BF),
+            pltpu.VMEM((HD, 2 * HD), F32),
+            pltpu.SemaphoreType.DMA((2, N_OUT + 1)),
+        ],
+        compiler_params=pltpu.CompilerParams(vmem_limit_bytes=60 * 2**20),
+    )(*results)
 
 
 def solution(mesh):

time: 114 us -> 113 us (level)
  local copies, waits for them, and re-layouts: 3.79 us -> 0 us
  Pallas kernels: 109 us -> 112 us
    unnamed x4 -> x0, local copies, waits for them, and re-layouts: 3.79 us -> none
    pallas_call x0 -> x1, Pallas kernels: none -> 2.47 us  [on_device(): pl.pallas_call(hand_out, out_shape=(jax.ShapeDtypeStruct((own, model), BF...]
where the time goes in v5:
time: 113 us; the launch traced here: 112 us
  Pallas kernels  112 us (99%)
    pallas_call x1, Pallas kernels, on_device(): pl.pallas_call(kernel, out_shape=(jax.ShapeDtypeStruct((own, model), BF),...  109 us
    pallas_call x1, Pallas kernels, on_device(): pl.pallas_call(hand_out, out_shape=(jax.ShapeDtypeStruct((own, model), BF...  2.47 us

profile of v5, /device:TPU:8, one launch (start us, length us, event | category | flops | bytes accessed | tf_op | source)
XLA Modules:
  0.0 112.4 jit_solution(15794644548496413353)
XLA Ops:
  0.6 109.3 %shard_map.122 = (bf16[128,8192]{1,0:T(8,128)(2,1)}, f32[128,256]{1,0:T(8,128)}) custom-call(bf16[128,8192]{1,0:T(8,128)(2,1)} %grad_out.1, bf16[512,256]{1,0:T(8,128)(2,1)} %queries_in.1, bf16[512,256]{1,0:T(8,128)(2,1)} %attended_in.1, bf16[512,128]{1,0:T(8,128)(2,1)} %keys_in.1, bf16[512,128]{1,0:T(8,128)(2,1)} %values_in.1, f32[2,512]{1,0:T(2,128)} %log_sums_in.1, ...), custom_call_target="tpu_custom_call" | custom-call | tf_op jit(solution)/shard_map/pallas_call | solution.py:594
  109.9 2.5 %shard_map.123 = (bf16[128,8192]{1,0:T(8,128)(2,1)}, f32[128,256]{1,0:T(8,128)}) custom-call(bf16[128,8192]{1,0:T(8,128)(2,1)} %get-tuple-element.4.gin, f32[128,256]{1,0:T(8,128)} %get-tuple-element.5.dwo), custom_call_target="tpu_custom_call" | custom-call | tf_op jit(solution)/shard_map/pallas_call | solution.py:639
